TPU v7x, 256 devices: a whole 4x4x8 slice. The times are simulated.
256 devices in a mesh: tx: 4 (over z_lo, core), img: 64 (over y, z_hi, x).
Axes of the slice: x: 4, y: 4, z: 8 (z_hi: 4, z_lo: 2; z = z_hi * 2 + z_lo), core: 2. Of those that a mesh axis runs over, the one named last changes fastest.
Arguments:
- encoded: bfloat16 [1024, 1024, 512], P('tx', 'img'), may hold values from -6 to 6
- signs: int32 [1024, 64], replicated, may hold values from -1 to 1, as said below
- tx_block: int32 [64, 16384], P('tx'), may hold values from 0 to 1
- rx_block: int32 [1024, 16384], P(None, 'img'), may hold values from 0 to 2
- apodization: int32 [1024, 16384], P(None, 'img'), may hold values 0 or 1
Outputs:
- image: float32 [16384, 128], P('img', 'tx')
Inputs may be any that keep to these rules, and one draw needn't show every extreme that they name: `signs`: every entry is 1 or -1. The columns are 64 distinct columns of the Sylvester Hadamard matrix of order 1024, every row multiplied by its own sign, so that two different columns are orthogonal.
All inputs are finite; a program needn't handle non-finite values. No bound on the sum of `apodization` on one device may be relied on, other than what follows from the above.
Results may differ from a plain program's by a relative error of at most 0.0029.
Values may be sent and summed in bfloat16 or wider, within the bound.
A program may use at most 192 MiB of HBM per device.

v0:
```python
import math
import jax
import jax.numpy as jnp
from jax import lax
from jax.sharding import PartitionSpec as P

E = 1024
K = 64
R = 1024
L = 128


def weights_for(rx_rows, mask_rows, tx_rows, block_count):
    total_block = tx_rows.T[:, :, None] + rx_rows.T[:, None, :]
    levels = jnp.arange(block_count, dtype=jnp.int32)
    chosen = total_block[..., None] == levels
    weight = jnp.where(
        chosen, mask_rows.T[:, None, :, None].astype(jnp.bfloat16), jnp.zeros((), jnp.bfloat16)
    )
    return weight.reshape(weight.shape[0], -1)


def on_device(encoded, signs, tx_block, rx_block, apodization):
    events_here, receivers_here, sample_count = encoded.shape
    transmits_here = tx_block.shape[0]
    lines_here = rx_block.shape[1]
    block_count = sample_count // L
    tx_index = lax.axis_index("tx")
    img_index = lax.axis_index("img")
    sign_cols = lax.dynamic_slice_in_dim(
        signs, tx_index * transmits_here, transmits_here, 1
    ).astype(jnp.bfloat16)
    piece = lax.all_gather(encoded, "tx", axis=0, tiled=True)
    flat_piece = piece.reshape(piece.shape[0], -1)
    summed = lax.dot_general(
        sign_cols, flat_piece, (((0,), (0,)), ((), ())), preferred_element_type=jnp.float32
    )
    decoded = (
        (summed * (1.0 / E))
        .astype(jnp.bfloat16)
        .reshape(transmits_here, receivers_here, sample_count)
    )
    own_tx = lax.dynamic_slice_in_dim(tx_block, img_index * lines_here, lines_here, 1)
    weight = weights_for(rx_block, apodization, own_tx, block_count)
    image = jnp.dot(
        weight,
        lax.all_gather(decoded, "img", axis=1, tiled=True).reshape(-1, L),
        preferred_element_type=jnp.float32,
    )
    scale = math.sqrt(E / (K * R))
    return lax.psum_scatter(image * scale, "tx", scatter_dimension=1, tiled=True)


def solution(mesh):
    placed = (P("tx", "img", None), P(), P("tx", None), P(None, "img"), P(None, "img"))
    return jax.shard_map(
        on_device, mesh=mesh, in_specs=placed, out_specs=P("img", "tx"), check_vma=False
    )
```

profile of v0, /device:TPU:1, one launch (start us, length us, event | category | flops | bytes accessed | tf_op | source)
XLA Modules:
  0.0 436.7 jit_solution(3269793722373958199)
XLA Ops:
  6.5 0.0 copy-start
  6.5 0.0 all-gather.3.cloned.1.call-start
  6.5 0.7 all-gather.3.cloned.1.call-update
  7.3 0.0 all-gather.5.cloned.1.call-start
  7.3 159.8 %all-gather.3.cloned.1.call-done = bf16[1024,16,512]{2,1,0:T(8,128)(2,1)} async-done(((bf16[256,16,512]{2,1,0:T(8,128)(2,1)}), bf16[1024,16,512]{2,1,0:T(8,128)(2,1)}) %all-gather.3.cloned.1.call-update) | async-done | bytes 16777232 | tf_op jit(solution)/shard_map/all_gather | solution.py:33
  167.1 15.8 %copy.9 = bf16[128,8,16,512]{3,1,2,0:T(8,128)(2,1)S(1)} copy(bf16[128,8,16,512]{3,2,1,0:T(8,128)(2,1)} %bitcast.15) | data formatting | bytes 33554432
  183.0 0.0 copy-start.3
  183.0 0.0 copy-start.2
  183.0 3.3 fusion.1
  186.3 0.8 copy.10
  187.1 0.0 all-gather.5.cloned.1.call-update
  187.1 0.0 reduce-scatter.2.cloned.1.call-start
  187.1 0.0 copy-done
  187.2 0.0 copy-done.3
  187.2 0.1 convert_bitcast_fusion
  187.3 0.0 copy-done.2
  187.3 7.4 %broadcast_add_fusion = s32[256,16,1024]{0,2,1:T(8,128)} fusion(s32[256,1024]{0,1:T(8,128)S(1)} %bitcast.17, s32[256,16]{0,1:T(8,128)S(1)} %dynamic-slice_bitcast_fusion), kind=kLoop, calls=%fused_computation.4 | loop fusion | flops 4194304 | bytes 17842176 | tf_op jit(solution)/shard_map/add | solution.py:14
  194.7 21.2 %fusion = bf16[256,16,1024,4]{0,3,2,1:T(4,128)(2,1)} fusion(s32[256,16,1024]{0,2,1:T(8,128)} %broadcast_add_fusion, bf16[256,1024]{0,1:T(8,128)(2,1)S(1)} %convert_bitcast_fusion), kind=kLoop, calls=%fused_computation.1 | loop fusion | flops 33554432 | bytes 50855936 | tf_op jit(solution)/shard_map/jit(_where)/select_n | solution.py:17
  215.9 46.5 %select_n.22 = bf16[256,65536]{0,1:T(8,128)(2,1)} reshape(bf16[256,16,1024,4]{0,3,2,1:T(4,128)(2,1)} %fusion) | data formatting | bytes 67108864 | tf_op jit(solution)/shard_map/jit(_where)/select_n | solution.py:17
  262.4 86.7 %all-gather.5.cloned.1.call-done = bf16[16,1024,512]{2,1,0:T(8,128)(2,1)} async-done(((bf16[16,16,512]{2,1,0:T(8,128)(2,1)}), bf16[16,1024,512]{2,1,0:T(8,128)(2,1)}) %all-gather.5.cloned.1.call-update) | async-done | bytes 16777232 | tf_op jit(solution)/shard_map/all_gather | solution.py:47
  349.0 26.6 %reshape.55 = bf16[65536,128]{1,0:T(8,128)(2,1)} reshape(bf16[16,1024,512]{2,1,0:T(8,128)(2,1)} %all-gather.5.cloned.1.call-done) | data formatting | bytes 33554432 | tf_op jit(solution)/shard_map/reshape | solution.py:47
  375.7 0.0 copy-start.1
  375.7 18.7 %convolution_multiply_fusion.1 = f32[256,128]{0,1:T(8,128)} fusion(bf16[256,65536]{0,1:T(8,128)(2,1)} %select_n.22, bf16[65536,128]{1,0:T(8,128)(2,1)} %reshape.55), kind=kOutput, calls=%fused_computation.5 | convolution fusion | flops 4295000064 | bytes 50462720 | tf_op jit(solution)/shard_map/dot_general | solution.py:45
  394.4 0.0 reduce-scatter.2.cloned.1.call-update
  394.4 35.7 %reduce-scatter.2.cloned.1.call-done = f32[256,32]{0,1:T(8,128)} async-done(((f32[256,128]{0,1:T(8,128)}), f32[256,32]{0,1:T(8,128)}) %reduce-scatter.2.cloned.1.call-update) | async-done | bytes 32784 | tf_op jit(solution)/shard_map/reduce_scatter | solution.py:51
  430.2 0.0 copy-done.1
  (1 shorter events, 0.0 us)
Async XLA Ops:
  6.5 180.6 %copy-start = (s32[16,16384]{1,0:T(8,128)S(1)}, s32[16,16384]{1,0:T(8,128)}, u32[]{:S(2)}) copy-start(s32[16,16384]{1,0:T(8,128)} %param.7) | copy-start | bytes 3145732
  6.5 160.6 %all-gather.3.cloned.1.call-start = ((), (), s32[]{:S(2)}) async-start(), calls=%async_computation.1 | async-start | bytes 20971520 | tf_op jit(solution)/shard_map/all_gather | solution.py:33
  7.3 341.8 %all-gather.5.cloned.1.call-start = ((), (), s32[]{:S(2)}) async-start(), calls=%async_computation.2 | async-start | bytes 17039360 | tf_op jit(solution)/shard_map/all_gather | solution.py:47
  183.0 4.2 copy-start.3
  183.0 4.3 copy-start.2
  187.1 243.1 %reduce-scatter.2.cloned.1.call-start = ((), (), s32[]{:S(2)}) async-start(), calls=%async_computation.3 | async-start | bytes 163840 | tf_op jit(solution)/shard_map/reduce_scatter | solution.py:51
  375.7 54.5 %copy-start.1 = (s32[16,16384]{1,0:T(8,128)S(1)}, s32[16,16384]{1,0:T(8,128)}, u32[]{:S(2)}) copy-start(s32[16,16384]{1,0:T(8,128)} %param.7) | copy-start | bytes 3145732
Sparse Core Ops, SparseCore 0:
  9.1 157.9 all-gather.2
  187.2 161.7 all-gather.4
  394.6 35.5 reduce-scatter.1
where the time goes:
time: 439 us; the launch traced here: 437 us
  waiting for transfers between devices  283 us (64%)
  local copies, waits for them, and re-layouts  89.8 us (20%)
  other arithmetic  28.7 us (7%)
  matrix products  22 us (5%)
  between operations  13.2 us (3%)
    all_gather x1, waiting for transfers between devices, on_device(): piece = lax.all_gather(encoded, 'tx', axis=0, tiled=True)  160 us
    all_gather x1, waiting for transfers between devices, on_device(): lax.all_gather(decoded, 'img', axis=1, tiled=True).reshape(-1, L)  86.7 us
    select_n x1, local copies, waits for them, and re-layouts, weights_for(): jnp.where(chosen, mask_rows.T[:, None, :, None].astype(jnp.bfloat16), jnp...  46.5 us
    reduce_scatter x1, waiting for transfers between devices, on_device(): lax.psum_scatter(image * scale, 'tx', scatter_dimension=1, tiled=True)  35.7 us
    reshape x1, local copies, waits for them, and re-layouts, on_device(): lax.all_gather(decoded, 'img', axis=1, tiled=True).reshape(-1, L)  26.6 us
    select_n x1, other arithmetic, weights_for(): jnp.where(chosen, mask_rows.T[:, None, :, None].astype(jnp.bfloat16), jnp...  21.2 us
    dot_general x1, matrix products, on_device(): jnp.dot(weight, lax.all_gather(decoded, 'img', axis=1, tiled=True).reshap...  18.7 us
    unnamed x10, local copies, waits for them, and re-layouts  16.7 us
  transfers between devices with their start and end apart: 3, of which 3 were waited for; matrix products, arithmetic and copies ran while one was open for 17% of the time, Pallas kernels for 0%

commit v1 on v0

--- a/solution.py
+++ b/solution.py
@@ -44,7 +44,9 @@
     weight = weights_for(rx_block, apodization, own_tx, block_count)
     image = jnp.dot(
         weight,
-        lax.all_gather(decoded, "img", axis=1, tiled=True).reshape(-1, L),
+        jnp.concatenate(
+            lax.all_to_all(jnp.stack([decoded] * lax.axis_size("img")), "img", 0, 0), axis=1
+        ).reshape(-1, L),
         preferred_element_type=jnp.float32,
     )
     scale = math.sqrt(E / (K * R))

time: 439 us -> 704 us (1.60)
  waiting for transfers between devices: 283 us -> 517 us
  local copies, waits for them, and re-layouts: 89.8 us -> 109 us
  starting transfers between devices: 0.08 us -> 12.1 us
    all_to_all x0 -> x1, waiting for transfers between devices: none -> 306 us  [on_device(): lax.all_to_all(jnp.stack([decoded] * lax.axis_size('img')), 'img', 0, 0)]
    all_gather x1 -> x0, waiting for transfers between devices: 86.7 us -> none  [on_device(): lax.all_gather(decoded, 'img', axis=1, tiled=True).reshape(-1, L)]
    another operation x0 -> x2, local copies, waits for them, and re-layouts: none -> 32.6 us  [the longest x1 26.6 us: on_device(): image = jnp.dot(weight, jnp.concatenate(lax.all_to_all(jnp.stack([decoded...]
    reduce_scatter x1, waiting for transfers between devices: 35.7 us -> 51 us  [on_device(): lax.psum_scatter(image * scale, 'tx', scatter_dimension=1, tiled=True)]
    reshape x1, local copies, waits for them, and re-layouts: 26.6 us -> 14 us  [on_device(): jnp.concatenate(lax.all_to_all(jnp.stack([decoded] * lax.axis_size('img')...]
    all_to_all x0 -> x1, starting transfers between devices: none -> 12.1 us  [on_device(): lax.all_to_all(jnp.stack([decoded] * lax.axis_size('img')), 'img', 0, 0)]
  transfers between devices with their start and end apart: 3 -> 3, of which waited for: 3 -> 3; matrix products, arithmetic and copies ran while one was open for 17% -> 11% of each run, Pallas kernels for 0% -> 0%
where the time goes in v1:
time: 704 us; the launch traced here: 702 us
  waiting for transfers between devices  517 us (73%)
  local copies, waits for them, and re-layouts  109 us (15%)
  other arithmetic  28.7 us (4%)
  matrix products  21.9 us (3%)
  between operations  13.5 us (2%)
  starting transfers between devices  12.1 us (2%)
    all_to_all x1, waiting for transfers between devices, on_device(): lax.all_to_all(jnp.stack([decoded] * lax.axis_size('img')), 'img', 0, 0)  306 us
    all_gather x1, waiting for transfers between devices, on_device(): piece = lax.all_gather(encoded, 'tx', axis=0, tiled=True)  160 us
    reduce_scatter x1, waiting for transfers between devices, on_device(): lax.psum_scatter(image * scale, 'tx', scatter_dimension=1, tiled=True)  51 us
    select_n x1, local copies, waits for them, and re-layouts, weights_for(): jnp.where(chosen, mask_rows.T[:, None, :, None].astype(jnp.bfloat16), jnp...  46.2 us
    another operation x1, local copies, waits for them, and re-layouts, on_device(): image = jnp.dot(weight, jnp.concatenate(lax.all_to_all(jnp.stack([decoded...  26.6 us
    select_n x1, other arithmetic, weights_for(): jnp.where(chosen, mask_rows.T[:, None, :, None].astype(jnp.bfloat16), jnp...  21.2 us
    dot_general x1, matrix products, on_device(): jnp.dot(weight, jnp.concatenate(lax.all_to_all(jnp.stack([decoded] * lax....  18.7 us
    unnamed x10, local copies, waits for them, and re-layouts  15.9 us
  transfers between devices with their start and end apart: 3, of which 3 were waited for; matrix products, arithmetic and copies ran while one was open for 11% of the time, Pallas kernels for 0%

profile of v1, /device:TPU:1, one launch (start us, length us, event | category | flops | bytes accessed | tf_op | source)
XLA Modules:
  0.0 702.3 jit_solution(7112774801244619966)
XLA Ops:
  6.5 0.0 copy-start
  6.5 0.0 all-gather.2.cloned.1.call-start
  6.5 0.7 all-gather.2.cloned.1.call-update
  7.3 159.9 %all-gather.2.cloned.1.call-done = bf16[1024,16,512]{2,1,0:T(8,128)(2,1)} async-done(((bf16[256,16,512]{2,1,0:T(8,128)(2,1)}), bf16[1024,16,512]{2,1,0:T(8,128)(2,1)}) %all-gather.2.cloned.1.call-update) | async-done | bytes 16777232 | tf_op jit(solution)/shard_map/all_gather | solution.py:33
  167.1 15.8 %copy.10 = bf16[128,8,16,512]{3,1,2,0:T(8,128)(2,1)S(1)} copy(bf16[128,8,16,512]{3,2,1,0:T(8,128)(2,1)} %bitcast.18) | data formatting | bytes 33554432
  183.0 3.1 fusion.1
  186.1 0.1 copy.11
  186.2 6.0 stack.3
  192.2 0.0 copy-start.3
  192.2 0.0 copy-start.2
  192.2 12.1 %all-to-all-start = ((bf16[64,16,16,512]{3,2,1,0:T(8,128)(2,1)}), bf16[64,16,16,512]{3,2,1,0:T(8,128)(2,1)}, u32[]{:S(2)}, u32[]{:S(2)}) async-start(bf16[64,16,16,512]{3,2,1,0:T(8,128)(2,1)} %stack.3), calls=%async_computation | async-start | bytes 33554432 | tf_op jit(solution)/shard_map/all_to_all | solution.py:48
  204.3 0.0 reduce-scatter.2.cloned.1.call-start
  204.3 0.0 copy-done
  204.4 0.0 copy-done.3
  204.4 0.1 convert_bitcast_fusion
  204.5 0.0 copy-done.2
  204.5 7.4 %broadcast_add_fusion = s32[256,16,1024]{0,2,1:T(8,128)} fusion(s32[256,1024]{0,1:T(8,128)S(1)} %bitcast.21, s32[256,16]{0,1:T(8,128)S(1)} %dynamic-slice_bitcast_fusion), kind=kLoop, calls=%fused_computation.4 | loop fusion | flops 4194304 | bytes 17842176 | tf_op jit(solution)/shard_map/add | solution.py:14
  211.8 21.2 %fusion = bf16[256,16,1024,4]{0,3,2,1:T(4,128)(2,1)} fusion(s32[256,16,1024]{0,2,1:T(8,128)} %broadcast_add_fusion, bf16[256,1024]{0,1:T(8,128)(2,1)S(1)} %convert_bitcast_fusion), kind=kLoop, calls=%fused_computation.1 | loop fusion | flops 33554432 | bytes 50855936 | tf_op jit(solution)/shard_map/jit(_where)/select_n | solution.py:17
  233.1 46.2 %select_n.22 = bf16[256,65536]{0,1:T(8,128)(2,1)} reshape(bf16[256,16,1024,4]{0,3,2,1:T(4,128)(2,1)} %fusion) | data formatting | bytes 67108864 | tf_op jit(solution)/shard_map/jit(_where)/select_n | solution.py:17
  279.2 305.9 %all-to-all-done = bf16[64,16,16,512]{3,2,1,0:T(8,128)(2,1)} async-done(((bf16[64,16,16,512]{3,2,1,0:T(8,128)(2,1)}), bf16[64,16,16,512]{3,2,1,0:T(8,128)(2,1)}, u32[]{:S(2)}, u32[]{:S(2)}) %all-to-all-start) | async-done | bytes 16777248 | tf_op jit(solution)/shard_map/all_to_all | solution.py:48
  585.1 14.0 %copy.9 = bf16[16,64,16,512]{3,2,1,0:T(8,128)(2,1)} copy(bf16[16,64,16,512]{3,2,0,1:T(8,128)(2,1)} %bitcast.3) | data formatting | bytes 33554432 | tf_op jit(solution)/shard_map/reshape | solution.py:47
  599.1 26.6 %reshape_reshape.3 = bf16[65536,128]{1,0:T(8,128)(2,1)} reshape(bf16[16,64,16,512]{3,2,1,0:T(8,128)(2,1)} %copy.9) | data formatting | bytes 33554432 | tf_op jit(solution)/shard_map/reshape;reshape | solution.py:49
  625.7 0.0 copy-start.1
  625.7 18.7 %convolution_multiply_fusion.1 = f32[256,128]{0,1:T(8,128)} fusion(bf16[256,65536]{0,1:T(8,128)(2,1)} %select_n.22, bf16[65536,128]{1,0:T(8,128)(2,1)} %reshape_reshape.3), kind=kOutput, calls=%fused_computation.5 | convolution fusion | flops 4295000064 | bytes 50462720 | tf_op jit(solution)/shard_map/dot_general | solution.py:45
  644.4 0.0 reduce-scatter.2.cloned.1.call-update
  644.5 51.0 %reduce-scatter.2.cloned.1.call-done = f32[256,32]{0,1:T(8,128)} async-done(((f32[256,128]{0,1:T(8,128)}), f32[256,32]{0,1:T(8,128)}) %reduce-scatter.2.cloned.1.call-update) | async-done | bytes 32784 | tf_op jit(solution)/shard_map/reduce_scatter | solution.py:53
  695.5 0.0 copy-done.1
  (1 shorter events, 0.0 us)
Async XLA Ops:
  6.5 197.8 %copy-start = (s32[16,16384]{1,0:T(8,128)S(1)}, s32[16,16384]{1,0:T(8,128)}, u32[]{:S(2)}) copy-start(s32[16,16384]{1,0:T(8,128)} %param.7) | copy-start | bytes 3145732
  6.5 160.6 %all-gather.2.cloned.1.call-start = ((), (), s32[]{:S(2)}) async-start(), calls=%async_computation.2 | async-start | bytes 20971520 | tf_op jit(solution)/shard_map/all_gather | solution.py:33
  192.2 12.2 %copy-start.3 = (s32[1024,256]{1,0:T(8,128)S(1)}, s32[1024,256]{1,0:T(8,128)}, u32[]{:S(2)}) copy-start(s32[1024,256]{1,0:T(8,128)} %param.9) | copy-start | bytes 3145732
  192.2 12.3 %copy-start.2 = (s32[1024,256]{1,0:T(8,128)S(1)}, s32[1024,256]{1,0:T(8,128)}, u32[]{:S(2)}) copy-start(s32[1024,256]{1,0:T(8,128)} %param.8) | copy-start | bytes 3145732
  192.2 392.9 %all-to-all-start = ((bf16[64,16,16,512]{3,2,1,0:T(8,128)(2,1)}), bf16[64,16,16,512]{3,2,1,0:T(8,128)(2,1)}, u32[]{:S(2)}, u32[]{:S(2)}) async-start(bf16[64,16,16,512]{3,2,1,0:T(8,128)(2,1)} %stack.3), calls=%async_computation | async-start | bytes 33554432 | tf_op jit(solution)/shard_map/all_to_all | solution.py:48
  204.3 491.2 %reduce-scatter.2.cloned.1.call-start = ((), (), s32[]{:S(2)}) async-start(), calls=%async_computation.3 | async-start | bytes 163840 | tf_op jit(solution)/shard_map/reduce_scatter | solution.py:53
  625.7 69.8 %copy-start.1 = (s32[16,16384]{1,0:T(8,128)S(1)}, s32[16,16384]{1,0:T(8,128)}, u32[]{:S(2)}) copy-start(s32[16,16384]{1,0:T(8,128)} %param.7) | copy-start | bytes 3145732
Sparse Core Ops, SparseCore 0:
  9.1 157.9 all-gather.1
  644.6 50.8 reduce-scatter.1
